TPU v7x, 32 devices: a whole 2x2x4 slice. The times are simulated.
32 devices in a mesh: expert: 4 (over y, core), dp: 8 (over z, x).
Axes of the slice: x: 2, y: 2, z: 4, core: 2. Of those that a mesh axis runs over, the one named last changes fastest.
Arguments:
- tokens: bfloat16 [2048, 3584], P(('dp', 'expert')), parts along dimension 0, may hold values from -6 to 6
- expert_ids: int32 [2048, 1], P(('dp', 'expert')), parts along dimension 0, may hold values from 0 to 3; in each aligned block of 64 rows (0 to 63, 64 to 127, ...) at most 18 rows name the same one
- combine: bfloat16 [2048, 1], P(('dp', 'expert')), parts along dimension 0, may hold values from 0.19921875 to 1
- w_gate: bfloat16 [3584, 8192], P(None, 'expert'), may hold values from -0.09375 to 0.09375
- w_up: bfloat16 [3584, 8192], P(None, 'expert'), may hold values from -0.09375 to 0.09375
- w_down: bfloat16 [8192, 3584], P('expert'), may hold values from -0.125 to 0.125
Outputs:
- mixed: bfloat16 [2048, 3584], P(('dp', 'expert')), parts along dimension 0
There are 8 independent parts, one for each index of `dp`. A program takes and returns all parts, laid end to end along the dimension named above; an argument that names none is the same for every part. Nothing has to cross between parts.
Inputs may be any that keep to these rules, and one draw needn't show every extreme that they name: `expert_ids`: each token names one expert. Among the 64 tokens of one device (aligned blocks of rows) no expert is named more than 18 times, a bound that some block reaches.
All inputs are finite; a program needn't handle non-finite values.
Results may differ from a plain program's by a relative error of at most 0.0057.
Values may be sent and summed in bfloat16 or wider, within the bound.
A program may use at most 128 MiB of HBM per device.

v0:
```python
import jax
import jax.numpy as jnp
from jax import lax
from jax.sharding import PartitionSpec as P

EXPERTS = 4
TOP = 1
CAP = 18


def local(tokens, expert_ids, combine, w_gate, w_up, w_down):
    devices = lax.axis_size("expert")
    span_size = devices // EXPERTS
    model_width = tokens.shape[1]
    token_count = tokens.shape[0]
    flat_ids = expert_ids.reshape(-1)
    labels = jnp.arange(EXPERTS, dtype=jnp.int32)
    member = (flat_ids[:, None] == labels[None, :]).astype(jnp.int32)
    rank_table = jnp.cumsum(member, axis=0) - 1
    positions = jnp.sum(member * rank_table, axis=1)
    slot_ids = jnp.arange(CAP, dtype=jnp.int32)
    placed = (member.T[:, None, :] == 1) & (positions[None, None, :] == slot_ids[None, :, None])
    repeated = jnp.repeat(tokens, TOP, axis=0)
    outgoing = jnp.einsum(
        "ecf,fd->ecd", placed.astype(jnp.bfloat16), repeated, preferred_element_type=jnp.float32
    ).astype(jnp.bfloat16)
    outgoing = jnp.repeat(outgoing, span_size, axis=0)
    arrived = lax.all_to_all(outgoing, "expert", split_axis=0, concat_axis=0, tiled=True)
    slot_count = arrived.shape[1]
    row_block = arrived.reshape(-1, model_width)
    gate_values = jnp.dot(row_block, w_gate, preferred_element_type=jnp.float32)
    up_values = jnp.dot(row_block, w_up, preferred_element_type=jnp.float32)
    hidden = (jax.nn.silu(gate_values) * up_values).astype(jnp.bfloat16)
    result = (
        jnp.dot(hidden, w_down, preferred_element_type=jnp.float32)
        .astype(jnp.bfloat16)
        .reshape(devices, slot_count, model_width)
    )
    returned_rows = lax.all_to_all(result, "expert", split_axis=0, concat_axis=0, tiled=True)
    summed = jnp.sum(
        returned_rows.astype(jnp.float32).reshape(EXPERTS, span_size, CAP, model_width), axis=1
    )
    weighted = placed.astype(jnp.float32) * combine.astype(jnp.float32).reshape(-1)[None, None, :]
    entry_rows = jnp.einsum("ecf,ecd->fd", weighted, summed, precision=lax.Precision.HIGHEST)
    mixed_rows = jnp.sum(entry_rows.reshape(token_count, TOP, model_width), axis=1)
    return mixed_rows.astype(jnp.bfloat16)


def solution(mesh):
    placed = (
        P(("dp", "expert"), None),
        P(("dp", "expert"), None),
        P(("dp", "expert"), None),
        P(None, "expert"),
        P(None, "expert"),
        P("expert", None),
    )
    return jax.shard_map(
        local, mesh=mesh, in_specs=placed, out_specs=P(("dp", "expert"), None), check_vma=False
    )
```

profile of v0, /device:TPU:0, one launch (start us, length us, event | category | flops | bytes accessed | tf_op | source)
XLA Modules:
  0.0 56.4 jit_solution(2965514269756863854)
XLA Ops:
  0.0 0.0 copy-start
  0.0 0.8 %fusion.5 = s32[64,4]{1,0:T(8,128)S(1)} fusion(s32[64]{0:T(128)} %bitcast.17), kind=kLoop, calls=%fused_computation.12 | loop fusion | flops 512 | bytes 1280 | tf_op jit(solution)/shard_map/convert_element_type | solution.py:18
  0.8 0.7 %convert_compare_fusion = pred[4,64]{1,0:T(4,128)(4,1)S(1)} fusion(s32[64]{0:T(128)} %bitcast.18), kind=kLoop, calls=%fused_computation.20 | loop fusion | flops 768 | bytes 512 | tf_op jit(solution)/shard_map/eq | solution.py:22
  1.4 0.1 reduce_window_sum.11
  1.5 0.8 %select_reduce_fusion = s32[64]{0:T(128)S(1)} fusion(s32[64,4]{1,0:T(8,128)S(1)} %reduce_window_sum.11, s32[64]{0:T(128)} %bitcast.19), kind=kLoop, calls=%fused_computation.10 | loop fusion | flops 960 | bytes 1536 | tf_op jit(solution)/shard_map/reduce_sum | solution.py:20
  2.4 0.0 copy-done
  2.4 0.3 convolution_convert_fusion
  2.7 14.6 %all_to_all.10 = bf16[4,18,3584]{2,1,0:T(8,128)(2,1)S(1)} all-to-all(bf16[4,18,3584]{2,1,0:T(8,128)(2,1)S(1)} %convolution_convert_fusion), channel_id=1, replica_groups=mesh['expert'=4,'dp'=8] {'expert'}, dimensions={0} | all-to-all | bytes 1032192 | tf_op jit(solution)/shard_map/all_to_all | solution.py:28
  17.4 0.2 reshape.60
  17.5 7.8 %fusion.14 = f32[72,2048]{1,0:T(8,128)S(1)} fusion(bf16[72,3584]{1,0:T(8,128)(2,1)S(1)} %reshape.60, bf16[3584,2048]{1,0:T(8,128)(2,1)} %param.9), kind=kOutput, calls=%fused_computation.25 | convolution fusion | flops 1056964608 | bytes 15785984 | tf_op jit(solution)/shard_map/dot_general | solution.py:31
  25.4 0.0 copy-start.1
  25.4 14.6 %convolution_convert_fusion.1 = bf16[72,3584]{1,0:T(8,128)(2,1)S(1)} fusion(bf16[2048,3584]{1,0:T(8,128)(2,1)} %param.11, bf16[72,3584]{1,0:T(8,128)(2,1)S(1)} %reshape.60, bf16[3584,2048]{1,0:T(8,128)(2,1)} %param.10, f32[72,2048]{1,0:T(8,128)S(1)} %fusion.14), kind=kOutput, calls=%fused_computation.2 | convolution fusion | flops 2115072000 | bytes 30982144 | tf_op jit(solution)/shard_map/dot_general | solution.py:35
  40.0 1.0 %reshape.61 = bf16[4,18,3584]{2,1,0:T(8,128)(2,1)} reshape(bf16[72,3584]{1,0:T(8,128)(2,1)S(1)} %convolution_convert_fusion.1) | data formatting | bytes 1032192 | tf_op jit(solution)/shard_map/reshape | solution.py:37
  41.0 3.5 %all-to-all-start.1 = ((bf16[4,18,3584]{2,1,0:T(8,128)(2,1)}), bf16[4,18,3584]{2,1,0:T(8,128)(2,1)S(1)}, u32[]{:S(2)}, u32[]{:S(2)}) async-start(bf16[4,18,3584]{2,1,0:T(8,128)(2,1)} %reshape.61), calls=%async_computation.1 | async-start | bytes 1376256 | tf_op jit(solution)/shard_map/all_to_all | solution.py:39
  44.5 0.0 copy-done.1
  44.5 10.5 %all-to-all-done.1 = bf16[4,18,3584]{2,1,0:T(8,128)(2,1)S(1)} async-done(((bf16[4,18,3584]{2,1,0:T(8,128)(2,1)}), bf16[4,18,3584]{2,1,0:T(8,128)(2,1)S(1)}, u32[]{:S(2)}, u32[]{:S(2)}) %all-to-all-start.1) | async-done | bytes 516128 | tf_op jit(solution)/shard_map/all_to_all | solution.py:39
  55.0 1.4 %fusion = bf16[64,3584]{1,0:T(8,128)(2,1)} fusion(bf16[4,18,3584]{2,1,0:T(8,128)(2,1)S(1)} %all-to-all-done.1, f32[64]{0:T(128)S(1)} %bitcast_convert_fusion, pred[18,64]{1,0:T(8,128)(4,1)S(1)} %iota_compare_fusion.1, pred[4,64]{1,0:T(4,128)(4,1)S(1)} %convert_compare_fusion), kind=kOutput, calls=%fused_computation.3 | convolution fusion | flops 198419456 | bytes 976512 | tf_op jit(solution)/shard_map/ecf,ecd->fd/dot_general | solution.py:44
  (2 shorter events, 0.0 us)
Async XLA Ops:
  0.0 2.4 %copy-start = (bf16[64,3584]{1,0:T(8,128)(2,1)S(1)}, bf16[64,3584]{1,0:T(8,128)(2,1)}, u32[]{:S(2)}) copy-start(bf16[64,3584]{1,0:T(8,128)(2,1)} %param.6) | copy-start | bytes 1376260
  25.4 19.1 %copy-start.1 = (bf16[64,1]{0,1:T(2,128)(2,1)S(1)}, bf16[64,1]{0,1:T(2,128)(2,1)}, u32[]{:S(2)}) copy-start(bf16[64,1]{0,1:T(2,128)(2,1)} %param.8) | copy-start | bytes 388
  41.0 14.0 %all-to-all-start.1 = ((bf16[4,18,3584]{2,1,0:T(8,128)(2,1)}), bf16[4,18,3584]{2,1,0:T(8,128)(2,1)S(1)}, u32[]{:S(2)}, u32[]{:S(2)}) async-start(bf16[4,18,3584]{2,1,0:T(8,128)(2,1)} %reshape.61), calls=%async_computation.1 | async-start | bytes 1376256 | tf_op jit(solution)/shard_map/all_to_all | solution.py:39
where the time goes:
time: 56.7 us; the launch traced here: 56.4 us
  matrix products  24.1 us (43%)
  blocking collectives  14.6 us (26%)
  waiting for transfers between devices  10.5 us (19%)
  starting transfers between devices  3.48 us (6%)
  other arithmetic  2.38 us (4%)
  local copies, waits for them, and re-layouts  1.19 us (2%)
    all_to_all x1, blocking collectives, local(): lax.all_to_all(outgoing, 'expert', split_axis=0, concat_axis=0, tiled=True)  14.6 us
    dot_general x1, matrix products, local(): jnp.dot(hidden, w_down, preferred_element_type=jnp.float32)  14.6 us
    all_to_all x1, waiting for transfers between devices, local(): lax.all_to_all(result, 'expert', split_axis=0, concat_axis=0, tiled=True)  10.5 us
    dot_general x1, matrix products, local(): gate_values = jnp.dot(row_block, w_gate, preferred_element_type=jnp.float32)  7.85 us
    all_to_all x1, starting transfers between devices, local(): lax.all_to_all(result, 'expert', split_axis=0, concat_axis=0, tiled=True)  3.48 us
    dot_general x1, matrix products, local(): jnp.einsum('ecf,ecd->fd', weighted, summed, precision=lax.Precision.HIGHEST)  1.35 us
  transfers between devices with their start and end apart: 1, of which 1 were waited for; matrix products, arithmetic and copies ran while one was open for 0% of the time, Pallas kernels for 0%

commit v1 on v0

--- a/solution.py
+++ b/solution.py
@@ -6,6 +6,28 @@
 EXPERTS = 4
 TOP = 1
 CAP = 18
+
+
+def in_blocks(array, dim, peers):
+    before, after = (array.shape[:dim], array.shape[dim + 1 :])
+    return jnp.moveaxis(array.reshape(*before, peers, -1, *after), dim, 0)
+
+
+def in_order(blocks, dim):
+    blocks = jnp.moveaxis(blocks, 0, dim)
+    lengths = blocks.shape
+    return blocks.reshape(*lengths[:dim], lengths[dim] * lengths[dim + 1], *lengths[dim + 2 :])
+
+
+def swapped_with_each(x, axis, split_dim, concat_dim):
+    length, index = (lax.axis_size(axis), lax.axis_index(axis))
+    parts = in_blocks(x, split_dim, length)
+    outs = [parts[index]]
+    for step in range(1, length):
+        sent = parts[index ^ step]
+        outs.append(lax.ppermute(sent, axis, [(i, i ^ step) for i in range(length)]))
+    parts = jnp.stack(outs)[index ^ jnp.arange(length)]
+    return in_order(parts, concat_dim)
 
 
 def local(tokens, expert_ids, combine, w_gate, w_up, w_down):
@@ -25,7 +47,7 @@
         "ecf,fd->ecd", placed.astype(jnp.bfloat16), repeated, preferred_element_type=jnp.float32
     ).astype(jnp.bfloat16)
     outgoing = jnp.repeat(outgoing, span_size, axis=0)
-    arrived = lax.all_to_all(outgoing, "expert", split_axis=0, concat_axis=0, tiled=True)
+    arrived = swapped_with_each(outgoing, "expert", 0, 0)
     slot_count = arrived.shape[1]
     row_block = arrived.reshape(-1, model_width)
     gate_values = jnp.dot(row_block, w_gate, preferred_element_type=jnp.float32)

time: 56.7 us -> 54.3 us (0.958)
  blocking collectives: 14.6 us -> 0 us
  waiting for transfers between devices: 10.5 us -> 18.8 us
  starting transfers between devices: 3.48 us -> 6.66 us
  local copies, waits for them, and re-layouts: 1.19 us -> 1.87 us
    all_to_all x1 -> x0, blocking collectives: 14.6 us -> none  [local(): lax.all_to_all(outgoing, 'expert', split_axis=0, concat_axis=0, tiled=True)]
    ppermute x0 -> x3, waiting for transfers between devices: none -> 8.33 us  [swapped_with_each(): lax.ppermute(sent, axis, [(i, i ^ step) for i in range(length)])]
    ppermute x0 -> x3, starting transfers between devices: none -> 3.17 us  [swapped_with_each(): lax.ppermute(sent, axis, [(i, i ^ step) for i in range(length)])]
    gather x0 -> x1, local copies, waits for them, and re-layouts: none -> 0.59 us  [swapped_with_each(): parts = jnp.stack(outs)[index ^ jnp.arange(length)]]
  transfers between devices with their start and end apart: 1 -> 4, of which waited for: 1 -> 3; matrix products, arithmetic and copies ran while one was open for 0% -> 0% of each run, Pallas kernels for 0% -> 0%
where the time goes in v1:
time: 54.3 us; the launch traced here: 54.1 us
  matrix products  24.1 us (44%)
  waiting for transfers between devices  18.8 us (35%)
  starting transfers between devices  6.66 us (12%)
  other arithmetic  2.5 us (5%)
  local copies, waits for them, and re-layouts  1.87 us (3%)
    dot_general x1, matrix products, local(): jnp.dot(hidden, w_down, preferred_element_type=jnp.float32)  14.6 us
    all_to_all x1, waiting for transfers between devices, local(): lax.all_to_all(result, 'expert', split_axis=0, concat_axis=0, tiled=True)  10.5 us
    ppermute x3, waiting for transfers between devices, swapped_with_each(): lax.ppermute(sent, axis, [(i, i ^ step) for i in range(length)])  8.33 us
    dot_general x1, matrix products, local(): gate_values = jnp.dot(row_block, w_gate, preferred_element_type=jnp.float32)  7.84 us
    all_to_all x1, starting transfers between devices, local(): lax.all_to_all(result, 'expert', split_axis=0, concat_axis=0, tiled=True)  3.48 us
    ppermute x3, starting transfers between devices, swapped_with_each(): lax.ppermute(sent, axis, [(i, i ^ step) for i in range(length)])  3.17 us
    dot_general x1, matrix products, local(): jnp.einsum('ecf,ecd->fd', weighted, summed, precision=lax.Precision.HIGHEST)  1.35 us
  transfers between devices with their start and end apart: 4, of which 3 were waited for; matrix products, arithmetic and copies ran while one was open for 0% of the time, Pallas kernels for 0%

profile of v1, /device:TPU:0, one launch (start us, length us, event | category | flops | bytes accessed | tf_op | source)
XLA Modules:
  0.0 54.1 jit_solution(15778936134714178556)
XLA Ops:
  0.0 0.0 copy-start
  0.0 0.8 %fusion.5 = s32[64,4]{1,0:T(8,128)S(1)} fusion(s32[64]{0:T(128)} %bitcast.29), kind=kLoop, calls=%fused_computation.15 | loop fusion | flops 512 | bytes 1280 | tf_op jit(solution)/shard_map/convert_element_type | solution.py:40
  0.8 0.7 %convert_compare_fusion = pred[4,64]{1,0:T(4,128)(4,1)S(1)} fusion(s32[64]{0:T(128)} %bitcast.30), kind=kLoop, calls=%fused_computation.25 | loop fusion | flops 768 | bytes 512 | tf_op jit(solution)/shard_map/eq | solution.py:44
  1.4 0.1 reduce_window_sum.11
  1.5 0.8 %select_reduce_fusion = s32[64]{0:T(128)S(1)} fusion(s32[64,4]{1,0:T(8,128)S(1)} %reduce_window_sum.11, s32[64]{0:T(128)} %bitcast.31), kind=kLoop, calls=%fused_computation.13 | loop fusion | flops 960 | bytes 1536 | tf_op jit(solution)/shard_map/reduce_sum | solution.py:42
  2.4 0.3 convolution_convert_fusion
  2.7 0.1 dynamic-slice_bitcast_fusion
  2.8 0.6 %collective-permute-start = (bf16[1,18,3584]{2,1,0:T(8,128)(2,1)S(1)}, bf16[1,18,3584]{2,1,0:T(8,128)(2,1)S(1)}, u32[]{:S(2)}, u32[]{:S(2)}) collective-permute-start(bf16[1,18,3584]{2,1,0:T(8,128)(2,1)S(1)} %get-tuple-element.8), channel_id=1, source_target_pairs={{0,8},{8,0},{16,24},{24,16},{1,9},{9,1},{17,25},{25,17},{2,10},{10... | collective-permute-start | bytes 387080 | tf_op jit(solution)/shard_map/ppermute | solution.py:28
  3.4 2.6 %collective-permute-start.1 = (bf16[1,18,3584]{2,1,0:T(8,128)(2,1)S(1)}, bf16[1,18,3584]{2,1,0:T(8,128)(2,1)S(1)}, u32[]{:S(2)}, u32[]{:S(2)}) collective-permute-start(bf16[1,18,3584]{2,1,0:T(8,128)(2,1)S(1)} %get-tuple-element.7), channel_id=1, source_target_pairs={{0,16},{8,24},{16,0},{24,8},{1,17},{9,25},{17,1},{25,9},{2,18},{10... | collective-permute-start | bytes 387080 | tf_op jit(solution)/shard_map/ppermute | solution.py:28
  6.0 0.0 collective-permute-start.2
  6.0 0.0 collective-permute-done
  6.0 5.2 %collective-permute-done.1 = bf16[1,18,3584]{2,1,0:T(8,128)(2,1)S(1)} collective-permute-done((bf16[1,18,3584]{2,1,0:T(8,128)(2,1)S(1)}, bf16[1,18,3584]{2,1,0:T(8,128)(2,1)S(1)}, u32[]{:S(2)}, u32[]{:S(2)}) %collective-permute-start.1) | collective-permute-done | bytes 129056 | tf_op jit(solution)/shard_map/ppermute | solution.py:28
  11.2 3.2 %collective-permute-done.2 = bf16[1,18,3584]{2,1,0:T(8,128)(2,1)S(1)} collective-permute-done((bf16[1,18,3584]{2,1,0:T(8,128)(2,1)S(1)}, bf16[1,18,3584]{2,1,0:T(8,128)(2,1)S(1)}, u32[]{:S(2)}, u32[]{:S(2)}) %collective-permute-start.2) | collective-permute-done | bytes 129056 | tf_op jit(solution)/shard_map/ppermute | solution.py:28
  14.4 0.1 maximum_bitcast_fusion
  14.5 0.6 %gather_fusion = bf16[4,18,3584]{2,1,0:T(8,128)(2,1)S(1)} fusion(bf16[4,18,3584]{2,1,0:T(8,128)(2,1)S(1)} %maximum_bitcast_fusion, s32[1024]{0:T(1024)S(1)} %pad_clamp_fusion), kind=kCustom, calls=%fused_computation | custom fusion | bytes 1032208 | tf_op jit(solution)/shard_map/gather | solution.py:29
  15.1 0.2 reshape_reshape.3
  15.2 7.8 %fusion.15 = f32[72,2048]{1,0:T(8,128)S(1)} fusion(bf16[72,3584]{1,0:T(8,128)(2,1)S(1)} %reshape_reshape.3, bf16[3584,2048]{1,0:T(8,128)(2,1)} %param.9), kind=kOutput, calls=%fused_computation.34 | convolution fusion | flops 1056964608 | bytes 15785984 | tf_op jit(solution)/shard_map/dot_general | solution.py:53
  23.1 0.0 copy-start.1
  23.1 14.6 %convolution_convert_fusion.1 = bf16[72,3584]{1,0:T(8,128)(2,1)S(1)} fusion(bf16[2048,3584]{1,0:T(8,128)(2,1)} %param.11, bf16[72,3584]{1,0:T(8,128)(2,1)S(1)} %reshape_reshape.3, bf16[3584,2048]{1,0:T(8,128)(2,1)} %param.10, f32[72,2048]{1,0:T(8,128)S(1)} %fusion.15), kind=kOutput, calls=%fused_computation.3 | convolution fusion | flops 2115072000 | bytes 30982144 | tf_op jit(solution)/shard_map/dot_general | solution.py:57
  37.7 1.0 %reshape.80 = bf16[4,18,3584]{2,1,0:T(8,128)(2,1)} reshape(bf16[72,3584]{1,0:T(8,128)(2,1)S(1)} %convolution_convert_fusion.1) | data formatting | bytes 1032192 | tf_op jit(solution)/shard_map/reshape | solution.py:59
  38.7 3.5 %all-to-all-start = ((bf16[4,18,3584]{2,1,0:T(8,128)(2,1)}), bf16[4,18,3584]{2,1,0:T(8,128)(2,1)S(1)}, u32[]{:S(2)}, u32[]{:S(2)}) async-start(bf16[4,18,3584]{2,1,0:T(8,128)(2,1)} %reshape.80), calls=%async_computation | async-start | bytes 1376256 | tf_op jit(solution)/shard_map/all_to_all | solution.py:61
  42.2 0.0 copy-done.1
  42.2 10.5 %all-to-all-done = bf16[4,18,3584]{2,1,0:T(8,128)(2,1)S(1)} async-done(((bf16[4,18,3584]{2,1,0:T(8,128)(2,1)}), bf16[4,18,3584]{2,1,0:T(8,128)(2,1)S(1)}, u32[]{:S(2)}, u32[]{:S(2)}) %all-to-all-start) | async-done | bytes 516128 | tf_op jit(solution)/shard_map/all_to_all | solution.py:61
  52.8 1.4 %fusion = bf16[64,3584]{1,0:T(8,128)(2,1)} fusion(bf16[4,18,3584]{2,1,0:T(8,128)(2,1)S(1)} %all-to-all-done, f32[64]{0:T(128)S(1)} %bitcast_convert_fusion, pred[18,64]{1,0:T(8,128)(4,1)S(1)} %iota_compare_fusion.1, pred[4,64]{1,0:T(4,128)(4,1)S(1)} %convert_compare_fusion), kind=kOutput, calls=%fused_computation.4 | convolution fusion | flops 198419456 | bytes 976512 | tf_op jit(solution)/shard_map/ecf,ecd->fd/dot_general | solution.py:66
  (5 shorter events, 0.0 us)
Async XLA Ops:
  0.0 2.4 %copy-start = (bf16[64,3584]{1,0:T(8,128)(2,1)S(1)}, bf16[64,3584]{1,0:T(8,128)(2,1)}, u32[]{:S(2)}) copy-start(bf16[64,3584]{1,0:T(8,128)(2,1)} %param.6) | copy-start | bytes 1376260
  2.8 3.2 %collective-permute-start = (bf16[1,18,3584]{2,1,0:T(8,128)(2,1)S(1)}, bf16[1,18,3584]{2,1,0:T(8,128)(2,1)S(1)}, u32[]{:S(2)}, u32[]{:S(2)}) collective-permute-start(bf16[1,18,3584]{2,1,0:T(8,128)(2,1)S(1)} %get-tuple-element.8), channel_id=1, source_target_pairs={{0,8},{8,0},{16,24},{24,16},{1,9},{9,1},{17,25},{25,17},{2,10},{10... | collective-permute-start | bytes 387080 | tf_op jit(solution)/shard_map/ppermute | solution.py:28
  3.4 7.8 %collective-permute-start.1 = (bf16[1,18,3584]{2,1,0:T(8,128)(2,1)S(1)}, bf16[1,18,3584]{2,1,0:T(8,128)(2,1)S(1)}, u32[]{:S(2)}, u32[]{:S(2)}) collective-permute-start(bf16[1,18,3584]{2,1,0:T(8,128)(2,1)S(1)} %get-tuple-element.7), channel_id=1, source_target_pairs={{0,16},{8,24},{16,0},{24,8},{1,17},{9,25},{17,1},{25,9},{2,18},{10... | collective-permute-start | bytes 387080 | tf_op jit(solution)/shard_map/ppermute | solution.py:28
  6.0 8.4 %collective-permute-start.2 = (bf16[1,18,3584]{2,1,0:T(8,128)(2,1)S(1)}, bf16[1,18,3584]{2,1,0:T(8,128)(2,1)S(1)}, u32[]{:S(2)}, u32[]{:S(2)}) collective-permute-start(bf16[1,18,3584]{2,1,0:T(8,128)(2,1)S(1)} %get-tuple-element.6), channel_id=1, source_target_pairs={{0,24},{8,16},{16,8},{24,0},{1,25},{9,17},{17,9},{25,1},{2,26},{10... | collective-permute-start | bytes 387080 | tf_op jit(solution)/shard_map/ppermute | solution.py:28
  23.1 19.1 %copy-start.1 = (bf16[64,1]{0,1:T(2,128)(2,1)S(1)}, bf16[64,1]{0,1:T(2,128)(2,1)}, u32[]{:S(2)}) copy-start(bf16[64,1]{0,1:T(2,128)(2,1)} %param.8) | copy-start | bytes 388
  38.7 14.0 %all-to-all-start = ((bf16[4,18,3584]{2,1,0:T(8,128)(2,1)}), bf16[4,18,3584]{2,1,0:T(8,128)(2,1)S(1)}, u32[]{:S(2)}, u32[]{:S(2)}) async-start(bf16[4,18,3584]{2,1,0:T(8,128)(2,1)} %reshape.80), calls=%async_computation | async-start | bytes 1376256 | tf_op jit(solution)/shard_map/all_to_all | solution.py:61
